TPU v7x, 32 devices: a whole 2x2x4 slice. The times are simulated.
32 devices in a mesh: row: 8 (over z, y), col: 4 (over x, core).
Axes of the slice: x: 2, y: 2, z: 4, core: 2. Of those that a mesh axis runs over, the one named last changes fastest.
Arguments:
- queries: bfloat16 [1024, 1024], P('row', 'col'), may hold values from -26 to 26
- key_vectors: bfloat16 [1024, 1024], P('row', 'col'), may hold values from -8 to 8
- values: bfloat16 [1024, 1024], P('row', 'col'), may hold values from -6 to 6
- sink_logit: float32 [8], P('col'), may hold values from -1 to 5
- lengths: int32 [8], replicated, may hold values from 1 to 576, as said below
- stream: bfloat16 [1024, 2048], P('row', 'col'), may hold values from -60 to 60
- out_weight: bfloat16 [1024, 2048], P('col', 'row'), may hold values from -0.1875 to 0.1875
- norm_gain: bfloat16 [2048], P('col'), may hold values from 0.25 to 1.75
- shared_gate: bfloat16 [2048, 2816], P('row', 'col'), may hold values from -0.125 to 0.125
- shared_up: bfloat16 [2048, 2816], P('row', 'col'), may hold values from -0.125 to 0.125
- shared_down: bfloat16 [2816, 2048], P('col', 'row'), may hold values from -0.109375 to 0.109375
- shared_switch: bfloat16 [2048], replicated, may hold values from -0.125 to 0.125
- expert_gate: bfloat16 [8, 2048, 1408], P('row', None, 'col'), may hold values from -0.125 to 0.125
- expert_up: bfloat16 [8, 2048, 1408], P('row', None, 'col'), may hold values from -0.125 to 0.125
- expert_down: bfloat16 [8, 1408, 2048], P('row', 'col'), may hold values from -0.15625 to 0.15625
- routes: int32 [1024, 4], P('row'), may hold values from 0 to 7, all different within a row; in each aligned block of 128 rows (0 to 127, 128 to 255, ...) at most 96 rows name the same one
- route_weights: float32 [1024, 4], P('row'), may hold values from 0.05 to 0.6
Outputs:
- attended: bfloat16 [1024, 1024], P('row', 'col')
- layer_out: bfloat16 [1024, 2048], P('row', 'col')
Inputs may be any that keep to these rules, and one draw needn't show every extreme that they name: `routes`: each row names 4 different experts; among the 128 rows of one device (aligned blocks) no expert is named more than 96 times, a bound that some block reaches. The lengths sum to 1024; exactly one prompt has 576 tokens.
All inputs are finite; a program needn't handle non-finite values.
Results may differ from a plain program's by a relative error of at most 0.01.
Values may be sent and summed in bfloat16 or wider, within the bound.
A program may use at most 128 MiB of HBM per device.

v0:
```python
import math
import jax
import jax.numpy as jnp
from jax import lax
from jax.sharding import PartitionSpec as P

HDIM = 128
WINDOW = 4096
norm_eps = 1e-06
masked_score = -1e30


def lower_bounds(lengths, positions):
    doc_ends = jnp.cumsum(lengths)
    starts = doc_ends - lengths
    begun_docs = starts[None, :] <= positions[:, None]
    doc_start = jnp.max(jnp.where(begun_docs, starts[None, :], 0), axis=1)
    return jnp.maximum(doc_start, positions - WINDOW + 1)


def body(
    queries,
    key_vectors,
    values,
    sink_logit,
    lengths,
    stream,
    out_weight,
    norm_gain,
    shared_gate,
    shared_up,
    shared_down,
    shared_switch,
    expert_gate,
    expert_up,
    expert_down,
    routes,
    route_weights,
):
    local_tokens = queries.shape[0]
    feature_width = queries.shape[1]
    head_count = feature_width // HDIM
    my_row = lax.axis_index("row")
    positions = my_row * local_tokens + jnp.arange(local_tokens, dtype=jnp.int32)
    lower_bound = lower_bounds(lengths, positions)
    query_heads = queries.reshape(local_tokens, head_count, HDIM)
    score_scale = 1.0 / math.sqrt(HDIM)
    key_value = jnp.stack([key_vectors, values], 0)
    key_piece = lax.all_gather(key_value, "row", axis=1, tiled=True)
    row_max = jnp.broadcast_to(sink_logit[None, :], (local_tokens, head_count))
    denominator = jnp.ones((local_tokens, head_count), jnp.float32)
    numerator = jnp.zeros((local_tokens, head_count, HDIM), jnp.float32)
    needed = key_piece.shape[1]
    key_heads = key_piece[0].reshape(needed, head_count, HDIM)
    value_heads = key_piece[1].reshape(needed, head_count, HDIM)
    scores = (
        jnp.einsum("qhd,khd->qhk", query_heads, key_heads, preferred_element_type=jnp.float32)
        * score_scale
    )
    key_places = jnp.arange(needed, dtype=jnp.int32)
    visible = (
        (key_places[None, :] >= lower_bound[:, None]) & (key_places[None, :] <= positions[:, None])
    )[:, None, :]
    masked = jnp.where(visible, scores, masked_score)
    new_max = jnp.maximum(row_max, jnp.max(masked, axis=2))
    weight = jnp.where(visible, jnp.exp(masked - new_max[:, :, None]), 0.0)
    rescale = jnp.exp(row_max - new_max)
    denominator = denominator * rescale + jnp.sum(weight, axis=2)
    numerator = numerator * rescale[:, :, None] + jnp.einsum(
        "qhk,khd->qhd", weight.astype(jnp.bfloat16), value_heads, preferred_element_type=jnp.float32
    )
    final_max, denominator, numerator = (new_max, denominator, numerator)
    attended = (
        (numerator / denominator[:, :, None])
        .reshape(local_tokens, feature_width)
        .astype(jnp.bfloat16)
    )
    head_terms = jnp.dot(
        attended,
        lax.all_gather(out_weight, "row", axis=1, tiled=True),
        preferred_element_type=jnp.float32,
    )
    mixed_heads = lax.psum_scatter(
        head_terms.astype(jnp.bfloat16), "col", scatter_dimension=1, tiled=True
    ).astype(jnp.float32)
    hidden = (stream.astype(jnp.float32) + mixed_heads).astype(jnp.bfloat16)
    widened = hidden.astype(jnp.float32)
    full_width = lax.axis_size("col") * hidden.shape[1]
    squares = lax.psum(jnp.sum(widened * widened, axis=1), "col")
    row_scale = lax.rsqrt(squares / full_width + norm_eps)
    normed_part = (widened * row_scale[:, None] * norm_gain.astype(jnp.float32)).astype(
        jnp.bfloat16
    )
    normed = lax.all_gather(normed_part, "col", axis=1, tiled=True)
    gate_part = jnp.dot(
        normed,
        lax.all_gather(shared_gate, "row", axis=0, tiled=True),
        preferred_element_type=jnp.float32,
    )
    up_part = jnp.dot(
        normed,
        lax.all_gather(shared_up, "row", axis=0, tiled=True),
        preferred_element_type=jnp.float32,
    )
    shared_act = (jax.nn.silu(gate_part) * up_part).astype(jnp.bfloat16)
    shared_part = jnp.dot(
        shared_act,
        lax.all_gather(shared_down, "row", axis=1, tiled=True),
        preferred_element_type=jnp.float32,
    )
    switch = jax.nn.sigmoid(jnp.dot(normed, shared_switch, preferred_element_type=jnp.float32))
    row_count = lax.axis_size("row")
    fanout = routes.shape[1]
    model_width = normed.shape[1]
    capacity = max(2, min(local_tokens, 3 * local_tokens * fanout // (2 * row_count)))
    flat_routes = routes.reshape(-1)
    onehot = (flat_routes[:, None] == jnp.arange(row_count, dtype=jnp.int32)[None, :]).astype(
        jnp.int32
    )
    before = jnp.cumsum(onehot, axis=0) - onehot
    slot_index = jnp.sum(before * onehot, axis=1)
    target = flat_routes * capacity + slot_index
    owner_row = jnp.arange(local_tokens * fanout, dtype=jnp.int32) // fanout
    source = jnp.full((row_count * capacity,), local_tokens, jnp.int32).at[target].set(owner_row)
    padded = jnp.concatenate([normed, jnp.zeros((1, model_width), jnp.bfloat16)], 0)
    outgoing = padded[source].reshape(row_count, capacity, model_width)
    received = lax.all_to_all(outgoing, "row", split_axis=0, concat_axis=0, tiled=True)
    senders, slot_count, received_width = received.shape
    dispatched = received.reshape(senders * slot_count, received_width)
    gate_out = jnp.dot(dispatched, expert_gate[0], preferred_element_type=jnp.float32)
    up_out = jnp.dot(dispatched, expert_up[0], preferred_element_type=jnp.float32)
    activation = (jax.nn.silu(gate_out) * up_out).astype(jnp.bfloat16)
    partial_out = jnp.dot(activation, expert_down[0], preferred_element_type=jnp.float32).astype(
        jnp.bfloat16
    )
    returned = lax.all_to_all(
        partial_out.reshape(senders, slot_count, received_width),
        "row",
        split_axis=0,
        concat_axis=0,
        tiled=True,
    )
    route_rows = returned.reshape(row_count * capacity, model_width)[target].reshape(
        local_tokens, fanout, model_width
    )
    routed = jnp.zeros((local_tokens, model_width), jnp.float32)
    for route_slot in range(fanout):
        routed = routed + route_weights[:, route_slot][:, None] * route_rows[
            :, route_slot, :
        ].astype(jnp.float32)
    layer_terms = switch[:, None] * shared_part + routed
    summed = lax.psum_scatter(
        layer_terms.astype(jnp.bfloat16), "col", scatter_dimension=1, tiled=True
    ).astype(jnp.float32)
    layer_out = (hidden.astype(jnp.float32) + summed).astype(jnp.bfloat16)
    return (attended, layer_out)


def solution(mesh):
    return jax.shard_map(
        body,
        mesh=mesh,
        in_specs=(
            P("row", "col"),
            P("row", "col"),
            P("row", "col"),
            P("col"),
            P(),
            P("row", "col"),
            P("col", "row"),
            P("col"),
            P("row", "col"),
            P("row", "col"),
            P("col", "row"),
            P(),
            P("row", None, "col"),
            P("row", None, "col"),
            P("row", "col", None),
            P("row", None),
            P("row", None),
        ),
        out_specs=(P("row", "col"), P("row", "col")),
        check_vma=False,
    )
```

profile of v0, /device:TPU:0, one launch (start us, length us, event | category | flops | bytes accessed | tf_op | source)
XLA Modules:
  0.0 430.8 jit_solution(6506192966484894538)
XLA Ops:
  7.2 1.1 copy.36
  8.3 1.0 copy.37
  9.3 0.7 pad_maximum_fusion
  10.0 0.7 all-gather.8.cloned.1.call-update
  10.8 0.8 reduce-window.19
  11.6 0.7 bitcast_subtract_fusion.1
  12.4 0.1 fusion.34
  12.5 40.4 %all-gather.6.cloned.1.call-done = bf16[2,1024,256]{1,2,0:T(8,128)(2,1)} async-done(((bf16[2,128,256]{1,2,0:T(8,128)(2,1)}), bf16[2,1024,256]{1,2,0:T(8,128)(2,1)}) %all-gather.6.cloned.1.call-update) | async-done | bytes 1048592 | tf_op jit(solution)/shard_map/all_gather | solution.py:49
  52.9 1.3 fusion.62
  54.2 0.4 fusion.63
  54.6 0.2 fusion.28
  55.0 0.4 fusion.18
  55.4 38.0 %all-gather.8.cloned.1.call-done = bf16[256,2048]{1,0:T(8,128)(2,1)} async-done(((bf16[256,256]{1,0:T(8,128)(2,1)}), bf16[256,2048]{1,0:T(8,128)(2,1)}) %all-gather.8.cloned.1.call-update) | async-done | bytes 1048592 | tf_op jit(solution)/shard_map/all_gather | solution.py:80
  93.4 2.4 convolution_convert_fusion.1
  95.9 0.5 all-gather.10.cloned.1.call-update
  96.4 0.1 copy.42
  96.6 0.1 eq.25
  96.8 1.1 reduce-window.20
  97.9 0.2 slice_reduce_fusion
  98.2 0.1 copy.41
  98.3 0.1 mul.135
  98.5 2.4 scatter_custom_fusion
  101.0 15.5 %reduce-scatter.3.cloned.1.call-done = bf16[128,512]{1,0:T(8,128)(2,1)} async-done(((bf16[128,2048]{1,0:T(8,128)(2,1)}), bf16[128,512]{1,0:T(8,128)(2,1)}) %reduce-scatter.3.cloned.1.call-update) | async-done | bytes 131088 | tf_op jit(solution)/shard_map/reduce_scatter | solution.py:83
  116.5 1.0 fusion.41
  117.5 5.8 %psum.7 = f32[128]{0:T(128)S(1)} all-reduce(f32[128]{0:T(128)S(1)} %fusion.41), channel_id=1, replica_groups=mesh['row'=8,'col'=4] {'col'}, use_global_device_ids=true, to_apply=%region_6.7 | all-reduce | flops 128 | bytes 1024 | tf_op jit(solution)/shard_map/psum | solution.py:89
  123.3 1.0 fusion.43
  124.3 7.3 %all_gather.20 = bf16[128,2048]{1,0:T(8,128)(2,1)S(1)} all-gather(bf16[128,512]{1,0:T(8,128)(2,1)S(1)} %fusion.43), channel_id=1, replica_groups=mesh['row'=8,'col'=4] {'col'}, dimensions={1}, use_global_device_ids=true | all-gather | bytes 655360 | tf_op jit(solution)/shard_map/all_gather | solution.py:94
  131.7 4.3 gather_fusion
  135.9 5.5 %all-to-all-start = ((bf16[8,96,2048]{2,1,0:T(8,128)(2,1)}), bf16[8,96,2048]{2,1,0:T(8,128)(2,1)}, u32[]{:S(2)}, u32[]{:S(2)}) async-start(bf16[8,96,2048]{2,1,0:T(8,128)(2,1)} %bitcast.109), calls=%async_computation.1 | async-start | bytes 6291456 | tf_op jit(solution)/shard_map/all_to_all | solution.py:127
  141.5 0.5 all-gather.12.cloned.1.call-update
  142.1 94.2 %all-to-all-done = bf16[8,96,2048]{2,1,0:T(8,128)(2,1)} async-done(((bf16[8,96,2048]{2,1,0:T(8,128)(2,1)}), bf16[8,96,2048]{2,1,0:T(8,128)(2,1)}, u32[]{:S(2)}, u32[]{:S(2)}) %all-to-all-start) | async-done | bytes 3145760 | tf_op jit(solution)/shard_map/all_to_all | solution.py:127
  236.2 4.7 %fusion.5 = f32[768,352]{0,1:T(8,128)} fusion(bf16[768,2048]{1,0:T(8,128)(2,1)} %bitcast.16, bf16[1,2048,352]{1,2,0:T(8,128)(2,1)} %param.29), kind=kOutput, calls=%fused_computation.11 | convolution fusion | flops 1107296256 | bytes 5668864 | tf_op jit(solution)/shard_map/dot_general | solution.py:130
  240.9 8.0 %convolution_convert_fusion = bf16[768,2048]{1,0:T(8,128)(2,1)} fusion(bf16[1,352,2048]{2,1,0:T(8,128)(2,1)S(1)} %copy-done, bf16[768,2048]{1,0:T(8,128)(2,1)} %bitcast.16, bf16[1,2048,352]{1,2,0:T(8,128)(2,1)} %param.30, f32[768,352]{0,1:T(8,128)} %fusion.5), kind=kOutput, calls=%fused_computation.3 | convolution fusion | flops 2217787392 | bytes 10256384 | tf_op jit(solution)/shard_map/dot_general | solution.py:133
  248.9 4.6 %all-to-all-start.1 = ((bf16[8,96,2048]{2,1,0:T(8,128)(2,1)}), bf16[8,96,2048]{2,1,0:T(8,128)(2,1)}, u32[]{:S(2)}, u32[]{:S(2)}) async-start(bf16[8,96,2048]{2,1,0:T(8,128)(2,1)} %bitcast.110), calls=%async_computation.2 | async-start | bytes 6291456 | tf_op jit(solution)/shard_map/all_to_all | solution.py:136
  253.6 0.5 all-gather.14.cloned.1.call-update
  254.1 0.2 reduce-scatter.5.cloned.1.call-start
  254.4 0.5 slice_bitcast_fusion.3
  254.9 0.3 fusion.22
  255.1 3.5 fusion.64
  258.6 92.9 %all-to-all-done.1 = bf16[8,96,2048]{2,1,0:T(8,128)(2,1)} async-done(((bf16[8,96,2048]{2,1,0:T(8,128)(2,1)}), bf16[8,96,2048]{2,1,0:T(8,128)(2,1)}, u32[]{:S(2)}, u32[]{:S(2)}) %all-to-all-start.1) | async-done | bytes 3145760 | tf_op jit(solution)/shard_map/all_to_all | solution.py:136
  351.5 7.5 %gather_fusion.1 = bf16[512,2048]{1,0:T(8,128)(2,1)} fusion(bf16[768,2048]{1,0:T(8,128)(2,1)} %bitcast.21, s32[1024]{0:T(1024)S(1)} %pad_clamp_fusion), kind=kCustom, calls=%fused_computation.1 | custom fusion | bytes 4196352 | tf_op jit(solution)/shard_map/gather | solution.py:143
  359.0 2.7 reshape.220
  361.8 4.5 %fusion.61 = (bf16[128,1,2048]{2,1,0:T(2,128)(2,1)}, bf16[128,1,2048]{2,1,0:T(2,128)(2,1)}, bf16[128,1,2048]{2,1,0:T(2,128)(2,1)}, bf16[128,1,2048]{2,1,0:T(2,128)(2,1)}) fusion(bf16[128,4,2048]{2,1,0:T(4,128)(2,1)S(1)} %reshape.220), kind=kLoop, calls=%fused_computation.104 | loop fusion | bytes 4194304 | tf_op jit(solution)/shard_map/slice | solution.py:148
  366.3 27.9 %all-gather.14.cloned.1.call-done = bf16[704,2048]{1,0:T(8,128)(2,1)} async-done(((bf16[704,256]{1,0:T(8,128)(2,1)}), bf16[704,2048]{1,0:T(8,128)(2,1)}) %all-gather.14.cloned.1.call-update) | async-done | bytes 2883600 | tf_op jit(solution)/shard_map/all_gather | solution.py:108
  394.2 8.1 %fusion.1 = bf16[128,2048]{1,0:T(8,128)(2,1)} fusion(bf16[704,2048]{1,0:T(8,128)(2,1)} %all-gather.14.cloned.1.call-done, bf16[128,2048]{1,0:T(8,128)(2,1)} %copy-done.1, bf16[2048,704]{0,1:T(8,128)(2,1)} %all-gather.12.cloned.1.call-done, bf16[128,1,2048]{2,1,0:T(2,128)(2,1)} %get-tuple-element.11, bf16[128,1,2048]{2,1,0:T(2,128)(2,1)} %get-tuple-element.9, ...), kind=kOutput, calls=%fused_computation.6 | convolution fusion | flops 742408192 | bytes 9275904 | tf_op jit(solution)/shard_map/dot_general | solution.py:106
  402.3 0.7 copy.48
  403.1 19.3 %reduce-scatter.5.cloned.1.call-done = bf16[128,512]{1,0:T(8,128)(2,1)} async-done(((bf16[128,2048]{1,0:T(8,128)(2,1)}), bf16[128,512]{1,0:T(8,128)(2,1)}) %reduce-scatter.5.cloned.1.call-update) | async-done | bytes 131088 | tf_op jit(solution)/shard_map/reduce_scatter | solution.py:152
  422.3 1.6 fusion.44
  (57 shorter events, 0.9 us)
Async XLA Ops:
  7.2 233.7 %copy-start = (bf16[1,352,2048]{2,1,0:T(8,128)(2,1)S(1)}, bf16[1,352,2048]{2,1,0:T(8,128)(2,1)}, u32[]{:S(2)}) copy-start(bf16[1,352,2048]{2,1,0:T(8,128)(2,1)} %param.31) | copy-start | bytes 4325380
  7.2 47.0 %copy-start.7 = (bf16[128,256]{1,0:T(8,128)(2,1)S(1)}, bf16[128,256]{1,0:T(8,128)(2,1)}, u32[]{:S(2)}) copy-start(bf16[128,256]{1,0:T(8,128)(2,1)} %param.17) | copy-start | bytes 196612
  7.2 45.7 %all-gather.6.cloned.1.call-start = ((), (), s32[]{:S(2)}) async-start(), calls=%async_computation.4 | async-start | bytes 1179648 | tf_op jit(solution)/shard_map/all_gather | solution.py:49
  10.0 44.6 %copy-start.10 = (f32[2]{0:T(128)S(1)}, f32[2]{0:T(128)}, u32[]{:S(2)}) copy-start(f32[2]{0:T(128)} %param.20) | copy-start | bytes 28
  10.0 83.4 %all-gather.8.cloned.1.call-start = ((), (), s32[]{:S(2)}) async-start(), calls=%async_computation.5 | async-start | bytes 1179648 | tf_op jit(solution)/shard_map/all_gather | solution.py:80
  10.7 105.8 %reduce-scatter.3.cloned.1.call-start = ((), (), s32[]{:S(2)}) async-start(), calls=%async_computation.6 | async-start | bytes 655360 | tf_op jit(solution)/shard_map/reduce_scatter | solution.py:83
  54.9 41.4 %copy-start.8 = (s32[128,4]{0,1:T(4,128)S(1)}, s32[128,4]{0,1:T(4,128)}, u32[]{:S(2)}) copy-start(s32[128,4]{0,1:T(4,128)} %param.32) | copy-start | bytes 6148
  54.9 41.8 %copy-start.12 = (bf16[512]{0:T(512)(128)(2,1)S(1)}, bf16[512]{0:T(512)(128)(2,1)}, u32[]{:S(2)}) copy-start(bf16[512]{0:T(512)(128)(2,1)} %param.24) | copy-start | bytes 3076
  55.3 40.5 %copy-start.5 = (bf16[128,2,128]{0,2,1:T(8,128)(2,1)}, bf16[128,2,128]{0,2,1:T(8,128)(2,1)S(1)}, u32[]{:S(2)}) copy-start(bf16[128,2,128]{0,2,1:T(8,128)(2,1)S(1)} %fusion.18) | copy-start | bytes 196612
  55.4 61.1 %copy-start.2 = (bf16[128,512]{1,0:T(8,128)(2,1)S(1)}, bf16[128,512]{1,0:T(8,128)(2,1)}, u32[]{:S(2)}) copy-start(bf16[128,512]{1,0:T(8,128)(2,1)} %param.22) | copy-start | bytes 393220
  95.8 159.3 %all-gather.10.cloned.1.call-start = ((), (), s32[]{:S(2)}) async-start(), calls=%async_computation.7 | async-start | bytes 3244032 | tf_op jit(solution)/shard_map/all_gather | solution.py:97
  131.6 123.5 %copy-start.1 = (bf16[128,2048]{1,0:T(8,128)(2,1)}, bf16[128,2048]{1,0:T(8,128)(2,1)S(1)}, u32[]{:S(2)}) copy-start(bf16[128,2048]{1,0:T(8,128)(2,1)S(1)} %all_gather.20) | copy-start | bytes 1572868
  135.9 100.3 %all-to-all-start = ((bf16[8,96,2048]{2,1,0:T(8,128)(2,1)}), bf16[8,96,2048]{2,1,0:T(8,128)(2,1)}, u32[]{:S(2)}, u32[]{:S(2)}) async-start(bf16[8,96,2048]{2,1,0:T(8,128)(2,1)} %bitcast.109), calls=%async_computation.1 | async-start | bytes 6291456 | tf_op jit(solution)/shard_map/all_to_all | solution.py:127
  141.5 224.8 %all-gather.12.cloned.1.call-start = ((), (), s32[]{:S(2)}) async-start(), calls=%async_computation.8 | async-start | bytes 3244032 | tf_op jit(solution)/shard_map/all_gather | solution.py:102
  248.9 5.4 %copy-start.9 = (bf16[2048]{0:T(1024)(128)(2,1)S(1)}, bf16[2048]{0:T(1024)(128)(2,1)}, u32[]{:S(2)}) copy-start(bf16[2048]{0:T(1024)(128)(2,1)} %param.28) | copy-start | bytes 12292
  248.9 5.4 %copy-start.11 = (f32[128,4]{0,1:T(4,128)S(1)}, f32[128,4]{0,1:T(4,128)}, u32[]{:S(2)}) copy-start(f32[128,4]{0,1:T(4,128)} %param.33) | copy-start | bytes 6148
  248.9 102.6 %all-to-all-start.1 = ((bf16[8,96,2048]{2,1,0:T(8,128)(2,1)}), bf16[8,96,2048]{2,1,0:T(8,128)(2,1)}, u32[]{:S(2)}, u32[]{:S(2)}) async-start(bf16[8,96,2048]{2,1,0:T(8,128)(2,1)} %bitcast.110), calls=%async_computation.2 | async-start | bytes 6291456 | tf_op jit(solution)/shard_map/all_to_all | solution.py:136
  253.5 140.7 %all-gather.14.cloned.1.call-start = ((), (), s32[]{:S(2)}) async-start(), calls=%async_computation.9 | async-start | bytes 3244032 | tf_op jit(solution)/shard_map/all_gather | solution.py:108
  254.1 168.3 %reduce-scatter.5.cloned.1.call-start = ((), (), s32[]{:S(2)}) async-start(), calls=%async_computation.10 | async-start | bytes 655360 | tf_op jit(solution)/shard_map/reduce_scatter | solution.py:152
  394.2 8.1 %copy-start.6 = (bf16[128,2,128]{0,2,1:T(8,128)(2,1)S(1)}, bf16[128,2,128]{0,2,1:T(8,128)(2,1)}, u32[]{:S(2)}) copy-start(bf16[128,2,128]{0,2,1:T(8,128)(2,1)} %copy-done.5) | copy-start | bytes 196612
  394.2 28.1 %copy-start.3 = (bf16[128,512]{1,0:T(8,128)(2,1)S(1)}, bf16[128,512]{1,0:T(8,128)(2,1)}, u32[]{:S(2)}) copy-start(bf16[128,512]{1,0:T(8,128)(2,1)} %param.22) | copy-start | bytes 393220
  394.2 28.1 %copy-start.4 = (bf16[128,512]{1,0:T(8,128)(2,1)S(1)}, bf16[128,512]{1,0:T(8,128)(2,1)}, u32[]{:S(2)}) copy-start(bf16[128,512]{1,0:T(8,128)(2,1)} %reduce-scatter.3.cloned.1.call-done) | copy-start | bytes 393220
Sparse Core Ops, SparseCore 0:
  10.6 42.2 all-gather.5
  55.0 38.4 all-gather.7
  95.9 20.5 reduce-scatter.2
  118.6 109.6 all-gather.9
  230.3 102.7 all-gather.11
  335.3 58.9 all-gather.13
  402.4 19.8 reduce-scatter.4
where the time goes:
time: 431 us
  waiting for transfers between devices  330 us (77%)
  matrix products  27.7 us (6%)
  local copies, waits for them, and re-layouts  26.9 us (6%)
  between operations  14.4 us (3%)
  blocking collectives  13.1 us (3%)
  starting transfers between devices  10.6 us (2%)
  other arithmetic  7.72 us (2%)
    all_to_all x1, waiting for transfers between devices, body(): lax.all_to_all(outgoing, 'row', split_axis=0, concat_axis=0, tiled=True)  94.2 us
    all_to_all x1, waiting for transfers between devices, body(): lax.all_to_all(partial_out.reshape(senders, slot_count, received_width),...  92.9 us
    all_gather x1, waiting for transfers between devices, body(): key_piece = lax.all_gather(key_value, 'row', axis=1, tiled=True)  40.4 us
    all_gather x1, waiting for transfers between devices, body(): lax.all_gather(out_weight, 'row', axis=1, tiled=True)  38 us
    all_gather x1, waiting for transfers between devices, body(): lax.all_gather(shared_down, 'row', axis=1, tiled=True)  27.9 us
    reduce_scatter x1, waiting for transfers between devices, body(): lax.psum_scatter(layer_terms.astype(jnp.bfloat16), 'col', scatter_dimensi...  19.3 us
    reduce_scatter x1, waiting for transfers between devices, body(): lax.psum_scatter(head_terms.astype(jnp.bfloat16), 'col', scatter_dimensio...  15.5 us
  transfers between devices with their start and end apart: 9, of which 7 were waited for; matrix products, arithmetic and copies ran while one was open for 11% of the time, Pallas kernels for 0%

commit v1 on v0

--- a/solution.py
+++ b/solution.py
@@ -46,7 +46,24 @@
     query_heads = queries.reshape(local_tokens, head_count, HDIM)
     score_scale = 1.0 / math.sqrt(HDIM)
     key_value = jnp.stack([key_vectors, values], 0)
-    key_piece = lax.all_gather(key_value, "row", axis=1, tiled=True)
+
+    def solve_vector_by_axis(arr, d_out):
+        group_axis = "row"
+        axis_len = lax.axis_size(group_axis)
+        grid = [arr]
+        for no in range(axis_len - 1):
+            grid.append(
+                lax.ppermute(
+                    grid[-1],
+                    axis_name=group_axis,
+                    perm=[(j, (j + 1) % axis_len) for j in range(axis_len)],
+                )
+            )
+        o_now = jnp.concatenate(grid[::-1], axis=d_out)
+        row_out = lax.axis_index(group_axis)
+        return jnp.roll(o_now, (row_out + 1) * arr.shape[d_out], d_out)
+
+    key_piece = solve_vector_by_axis(key_value, 1)
     row_max = jnp.broadcast_to(sink_logit[None, :], (local_tokens, head_count))
     denominator = jnp.ones((local_tokens, head_count), jnp.float32)
     numerator = jnp.zeros((local_tokens, head_count, HDIM), jnp.float32)

time: 431 us -> 410 us (0.951)
  waiting for transfers between devices: 330 us -> 306 us
    ppermute x0 -> x7, waiting for transfers between devices: none -> 54.2 us  [solve_vector_by_axis(): lax.ppermute(grid[-1], axis_name=group_axis, perm=[(j, (j + 1) % axis_len...]
    all_gather x1 -> x0, waiting for transfers between devices: 40.4 us -> none  [body(): key_piece = lax.all_gather(key_value, 'row', axis=1, tiled=True)]
    all_gather x1, waiting for transfers between devices: 38 us -> 0.02 us  [body(): lax.all_gather(out_weight, 'row', axis=1, tiled=True)]
    all_gather x1, waiting for transfers between devices: 27.9 us -> 0.01 us  [body(): lax.all_gather(shared_down, 'row', axis=1, tiled=True)]
    all_gather x1, waiting for transfers between devices: 0.01 us -> 27.7 us  [body(): lax.all_gather(shared_up, 'row', axis=0, tiled=True)]
  transfers between devices with their start and end apart: 9 -> 15, of which waited for: 7 -> 12; matrix products, arithmetic and copies ran while one was open for 11% -> 11% of each run, Pallas kernels for 0% -> 0%
where the time goes in v1:
time: 410 us; the launch traced here: 409 us
  waiting for transfers between devices  306 us (75%)
  matrix products  27.7 us (7%)
  local copies, waits for them, and re-layouts  26.6 us (6%)
  between operations  14.5 us (4%)
  starting transfers between devices  13.5 us (3%)
  blocking collectives  13.1 us (3%)
  other arithmetic  7.13 us (2%)
    all_to_all x1, waiting for transfers between devices, body(): lax.all_to_all(outgoing, 'row', split_axis=0, concat_axis=0, tiled=True)  94.4 us
    all_to_all x1, waiting for transfers between devices, body(): lax.all_to_all(partial_out.reshape(senders, slot_count, received_width),...  93.1 us
    ppermute x7, waiting for transfers between devices, solve_vector_by_axis(): lax.ppermute(grid[-1], axis_name=group_axis, perm=[(j, (j + 1) % axis_len...  54.2 us
    all_gather x1, waiting for transfers between devices, body(): lax.all_gather(shared_up, 'row', axis=0, tiled=True)  27.7 us
    reduce_scatter x1, waiting for transfers between devices, body(): lax.psum_scatter(layer_terms.astype(jnp.bfloat16), 'col', scatter_dimensi...  19.2 us
    reduce_scatter x1, waiting for transfers between devices, body(): lax.psum_scatter(head_terms.astype(jnp.bfloat16), 'col', scatter_dimensio...  16 us
  transfers between devices with their start and end apart: 15, of which 12 were waited for; matrix products, arithmetic and copies ran while one was open for 11% of the time, Pallas kernels for 0%

profile of v1, /device:TPU:0, one launch (start us, length us, event | category | flops | bytes accessed | tf_op | source)
XLA Modules:
  0.0 408.9 jit_solution(3787224130375437808)
XLA Ops:
  7.2 1.1 copy.36
  8.3 1.0 copy.37
  9.3 3.0 collective-permute-start
  12.3 6.5 %collective-permute-done = bf16[2,128,256]{1,2,0:T(8,128)(2,1)S(1)} collective-permute-done((bf16[2,128,256]{1,2,0:T(8,128)(2,1)S(1)}, bf16[2,128,256]{1,2,0:T(8,128)(2,1)S(1)}, u32[]{:S(2)}, u32[]{:S(2)}) %collective-permute-start) | collective-permute-done | bytes 131104 | tf_op jit(solution)/shard_map/ppermute | solution.py:56
  18.8 7.7 %collective-permute-done.1 = bf16[2,128,256]{1,2,0:T(8,128)(2,1)S(1)} collective-permute-done((bf16[2,128,256]{1,2,0:T(8,128)(2,1)S(1)}, bf16[2,128,256]{1,2,0:T(8,128)(2,1)S(1)}, u32[]{:S(2)}, u32[]{:S(2)}) %collective-permute-start.1) | collective-permute-done | bytes 131104 | tf_op jit(solution)/shard_map/ppermute | solution.py:56
  26.6 0.8 reduce-window.19
  27.4 6.7 %collective-permute-done.2 = bf16[2,128,256]{1,2,0:T(8,128)(2,1)S(1)} collective-permute-done((bf16[2,128,256]{1,2,0:T(8,128)(2,1)S(1)}, bf16[2,128,256]{1,2,0:T(8,128)(2,1)S(1)}, u32[]{:S(2)}, u32[]{:S(2)}) %collective-permute-start.2) | collective-permute-done | bytes 131104 | tf_op jit(solution)/shard_map/ppermute | solution.py:56
  34.2 0.7 bitcast_subtract_fusion.1
  34.8 7.7 %collective-permute-done.3 = bf16[2,128,256]{1,2,0:T(8,128)(2,1)S(1)} collective-permute-done((bf16[2,128,256]{1,2,0:T(8,128)(2,1)S(1)}, bf16[2,128,256]{1,2,0:T(8,128)(2,1)S(1)}, u32[]{:S(2)}, u32[]{:S(2)}) %collective-permute-start.3) | collective-permute-done | bytes 131104 | tf_op jit(solution)/shard_map/ppermute | solution.py:56
  42.6 8.1 %collective-permute-done.4 = bf16[2,128,256]{1,2,0:T(8,128)(2,1)S(1)} collective-permute-done((bf16[2,128,256]{1,2,0:T(8,128)(2,1)S(1)}, bf16[2,128,256]{1,2,0:T(8,128)(2,1)S(1)}, u32[]{:S(2)}, u32[]{:S(2)}) %collective-permute-start.4) | collective-permute-done | bytes 131104 | tf_op jit(solution)/shard_map/ppermute | solution.py:56
  50.7 8.8 %collective-permute-done.5 = bf16[2,128,256]{1,2,0:T(8,128)(2,1)S(1)} collective-permute-done((bf16[2,128,256]{1,2,0:T(8,128)(2,1)S(1)}, bf16[2,128,256]{1,2,0:T(8,128)(2,1)S(1)}, u32[]{:S(2)}, u32[]{:S(2)}) %collective-permute-start.5) | collective-permute-done | bytes 131104 | tf_op jit(solution)/shard_map/ppermute | solution.py:56
  59.5 0.1 fusion.34
  59.6 8.7 %collective-permute-done.6 = bf16[2,128,256]{1,2,0:T(8,128)(2,1)S(1)} collective-permute-done((bf16[2,128,256]{1,2,0:T(8,128)(2,1)S(1)}, bf16[2,128,256]{1,2,0:T(8,128)(2,1)S(1)}, u32[]{:S(2)}, u32[]{:S(2)}) %collective-permute-start.6) | collective-permute-done | bytes 131104 | tf_op jit(solution)/shard_map/ppermute | solution.py:56
  69.2 0.3 copy-done.7
  69.5 0.4 fusion.62
  69.9 0.2 fusion.28
  70.3 0.4 fusion.18
  70.7 2.4 convolution_convert_fusion.1
  73.2 0.7 all-gather.7.cloned.1.call-update
  74.3 1.1 reduce-window.20
  75.4 0.2 slice_reduce_fusion
  76.0 2.4 scatter_custom_fusion
  78.5 16.0 %reduce-scatter.3.cloned.1.call-done = bf16[128,512]{1,0:T(8,128)(2,1)} async-done(((bf16[128,2048]{1,0:T(8,128)(2,1)}), bf16[128,512]{1,0:T(8,128)(2,1)}) %reduce-scatter.3.cloned.1.call-update) | async-done | bytes 131088 | tf_op jit(solution)/shard_map/reduce_scatter | solution.py:100
  94.5 1.0 fusion.41
  95.5 5.8 %psum.7 = f32[128]{0:T(128)S(1)} all-reduce(f32[128]{0:T(128)S(1)} %fusion.41), channel_id=1, replica_groups=mesh['row'=8,'col'=4] {'col'}, use_global_device_ids=true, to_apply=%region_6.7 | all-reduce | flops 128 | bytes 1024 | tf_op jit(solution)/shard_map/psum | solution.py:106
  101.3 1.0 fusion.43
  102.3 7.3 %all_gather.16 = bf16[128,2048]{1,0:T(8,128)(2,1)S(1)} all-gather(bf16[128,512]{1,0:T(8,128)(2,1)S(1)} %fusion.43), channel_id=1, replica_groups=mesh['row'=8,'col'=4] {'col'}, dimensions={1}, use_global_device_ids=true | all-gather | bytes 655360 | tf_op jit(solution)/shard_map/all_gather | solution.py:111
  109.7 4.2 %gather_fusion = bf16[768,2048]{1,0:T(8,128)(2,1)} fusion(bf16[129,2048]{1,0:T(8,128)(2,1)S(1)} %concatenate.10, s32[1024]{0:T(1024)S(1)} %pad_clamp_fusion.1), kind=kCustom, calls=%fused_computation | custom fusion | bytes 6294528 | tf_op jit(solution)/shard_map/gather | solution.py:143
  113.9 5.5 %all-to-all-start = ((bf16[8,96,2048]{2,1,0:T(8,128)(2,1)}), bf16[8,96,2048]{2,1,0:T(8,128)(2,1)}, u32[]{:S(2)}, u32[]{:S(2)}) async-start(bf16[8,96,2048]{2,1,0:T(8,128)(2,1)} %bitcast.109), calls=%async_computation.1 | async-start | bytes 6291456 | tf_op jit(solution)/shard_map/all_to_all | solution.py:144
  119.5 0.5 all-gather.11.cloned.1.call-update
  120.0 94.4 %all-to-all-done = bf16[8,96,2048]{2,1,0:T(8,128)(2,1)} async-done(((bf16[8,96,2048]{2,1,0:T(8,128)(2,1)}), bf16[8,96,2048]{2,1,0:T(8,128)(2,1)}, u32[]{:S(2)}, u32[]{:S(2)}) %all-to-all-start) | async-done | bytes 3145760 | tf_op jit(solution)/shard_map/all_to_all | solution.py:144
  214.4 4.7 %fusion.5 = f32[768,352]{0,1:T(8,128)} fusion(bf16[768,2048]{1,0:T(8,128)(2,1)} %bitcast.16, bf16[1,2048,352]{1,2,0:T(8,128)(2,1)} %param.29), kind=kOutput, calls=%fused_computation.11 | convolution fusion | flops 1107296256 | bytes 5668864 | tf_op jit(solution)/shard_map/dot_general | solution.py:147
  219.0 8.0 %convolution_convert_fusion = bf16[768,2048]{1,0:T(8,128)(2,1)} fusion(bf16[1,352,2048]{2,1,0:T(8,128)(2,1)S(1)} %copy-done, bf16[768,2048]{1,0:T(8,128)(2,1)} %bitcast.16, bf16[1,2048,352]{1,2,0:T(8,128)(2,1)} %param.30, f32[768,352]{0,1:T(8,128)} %fusion.5), kind=kOutput, calls=%fused_computation.3 | convolution fusion | flops 2217787392 | bytes 10256384 | tf_op jit(solution)/shard_map/dot_general | solution.py:150
  227.1 4.6 %all-to-all-start.1 = ((bf16[8,96,2048]{2,1,0:T(8,128)(2,1)}), bf16[8,96,2048]{2,1,0:T(8,128)(2,1)}, u32[]{:S(2)}, u32[]{:S(2)}) async-start(bf16[8,96,2048]{2,1,0:T(8,128)(2,1)} %bitcast.110), calls=%async_computation.2 | async-start | bytes 6291456 | tf_op jit(solution)/shard_map/all_to_all | solution.py:153
  231.7 0.5 all-gather.9.cloned.1.call-update
  232.2 0.2 reduce-scatter.5.cloned.1.call-start
  232.5 0.5 slice_bitcast_fusion.3
  233.0 0.3 fusion.22
  233.3 3.5 fusion.63
  236.8 93.1 %all-to-all-done.1 = bf16[8,96,2048]{2,1,0:T(8,128)(2,1)} async-done(((bf16[8,96,2048]{2,1,0:T(8,128)(2,1)}), bf16[8,96,2048]{2,1,0:T(8,128)(2,1)}, u32[]{:S(2)}, u32[]{:S(2)}) %all-to-all-start.1) | async-done | bytes 3145760 | tf_op jit(solution)/shard_map/all_to_all | solution.py:153
  329.8 7.5 %gather_fusion.1 = bf16[512,2048]{1,0:T(8,128)(2,1)} fusion(bf16[768,2048]{1,0:T(8,128)(2,1)} %bitcast.21, s32[1024]{0:T(1024)S(1)} %pad_clamp_fusion), kind=kCustom, calls=%fused_computation.1 | custom fusion | bytes 4196352 | tf_op jit(solution)/shard_map/gather | solution.py:160
  337.4 2.7 reshape.220
  340.1 4.5 %fusion.61 = (bf16[128,1,2048]{2,1,0:T(2,128)(2,1)}, bf16[128,1,2048]{2,1,0:T(2,128)(2,1)}, bf16[128,1,2048]{2,1,0:T(2,128)(2,1)}, bf16[128,1,2048]{2,1,0:T(2,128)(2,1)}) fusion(bf16[128,4,2048]{2,1,0:T(4,128)(2,1)S(1)} %reshape.220), kind=kLoop, calls=%fused_computation.122 | loop fusion | bytes 4194304 | tf_op jit(solution)/shard_map/slice | solution.py:165
  344.6 27.7 %all-gather.9.cloned.1.call-done = bf16[2048,704]{0,1:T(8,128)(2,1)} async-done(((bf16[256,704]{0,1:T(8,128)(2,1)}), bf16[2048,704]{0,1:T(8,128)(2,1)}) %all-gather.9.cloned.1.call-update) | async-done | bytes 2883600 | tf_op jit(solution)/shard_map/all_gather | solution.py:119
  372.3 8.1 %fusion.1 = bf16[128,2048]{1,0:T(8,128)(2,1)} fusion(bf16[704,2048]{1,0:T(8,128)(2,1)} %all-gather.11.cloned.1.call-done, bf16[128,2048]{1,0:T(8,128)(2,1)} %copy-done.1, bf16[2048,704]{0,1:T(8,128)(2,1)} %all-gather.9.cloned.1.call-done, bf16[128,1,2048]{2,1,0:T(2,128)(2,1)} %get-tuple-element.11, bf16[128,1,2048]{2,1,0:T(2,128)(2,1)} %get-tuple-element.9, ...), kind=kOutput, calls=%fused_computation.6 | convolution fusion | flops 742408192 | bytes 9275904 | tf_op jit(solution)/shard_map/dot_general | solution.py:123
  380.4 0.7 copy.48
  381.2 19.2 %reduce-scatter.5.cloned.1.call-done = bf16[128,512]{1,0:T(8,128)(2,1)} async-done(((bf16[128,2048]{1,0:T(8,128)(2,1)}), bf16[128,512]{1,0:T(8,128)(2,1)}) %reduce-scatter.5.cloned.1.call-update) | async-done | bytes 131088 | tf_op jit(solution)/shard_map/reduce_scatter | solution.py:169
  400.4 1.6 fusion.44
  (84 shorter events, 2.1 us)
Async XLA Ops:
  7.2 211.9 %copy-start = (bf16[1,352,2048]{2,1,0:T(8,128)(2,1)S(1)}, bf16[1,352,2048]{2,1,0:T(8,128)(2,1)}, u32[]{:S(2)}) copy-start(bf16[1,352,2048]{2,1,0:T(8,128)(2,1)} %param.31) | copy-start | bytes 4325380
  7.2 63.5 %all-gather.5.cloned.1.call-start = ((), (), s32[]{:S(2)}) async-start(), calls=%async_computation.4 | async-start | bytes 1179648 | tf_op jit(solution)/shard_map/all_gather | solution.py:97
  9.3 9.6 %collective-permute-start = (bf16[2,128,256]{1,2,0:T(8,128)(2,1)S(1)}, bf16[2,128,256]{1,2,0:T(8,128)(2,1)S(1)}, u32[]{:S(2)}, u32[]{:S(2)}) collective-permute-start(bf16[2,128,256]{1,2,0:T(8,128)(2,1)S(1)} %pad_maximum_fusion), channel_id=1, source_target_pairs={{0,4},{4,8},{8,12},{12,16},{16,20},{20,24},{24,28},{28,0},{1,5},{5... | collective-permute-start | bytes 393224 | tf_op jit(solution)/shard_map/ppermute | solution.py:56
  18.8 7.7 %collective-permute-start.1 = (bf16[2,128,256]{1,2,0:T(8,128)(2,1)S(1)}, bf16[2,128,256]{1,2,0:T(8,128)(2,1)S(1)}, u32[]{:S(2)}, u32[]{:S(2)}) collective-permute-start(bf16[2,128,256]{1,2,0:T(8,128)(2,1)S(1)} %collective-permute-done), channel_id=1, source_target_pairs={{0,4},{4,8},{8,12},{12,16},{16,20},{20,24},{24,28},{28,0},{1,5},{5... | collective-permute-start | bytes 393224 | tf_op jit(solution)/shard_map/ppermute | solution.py:56
  26.5 7.7 %collective-permute-start.2 = (bf16[2,128,256]{1,2,0:T(8,128)(2,1)S(1)}, bf16[2,128,256]{1,2,0:T(8,128)(2,1)S(1)}, u32[]{:S(2)}, u32[]{:S(2)}) collective-permute-start(bf16[2,128,256]{1,2,0:T(8,128)(2,1)S(1)} %collective-permute-done.1), channel_id=1, source_target_pairs={{0,4},{4,8},{8,12},{12,16},{16,20},{20,24},{24,28},{28,0},{1,5},{5... | collective-permute-start | bytes 393224 | tf_op jit(solution)/shard_map/ppermute | solution.py:56
  26.5 68.0 %reduce-scatter.3.cloned.1.call-start = ((), (), s32[]{:S(2)}) async-start(), calls=%async_computation.5 | async-start | bytes 655360 | tf_op jit(solution)/shard_map/reduce_scatter | solution.py:100
  34.2 8.3 %collective-permute-start.3 = (bf16[2,128,256]{1,2,0:T(8,128)(2,1)S(1)}, bf16[2,128,256]{1,2,0:T(8,128)(2,1)S(1)}, u32[]{:S(2)}, u32[]{:S(2)}) collective-permute-start(bf16[2,128,256]{1,2,0:T(8,128)(2,1)S(1)} %collective-permute-done.2), channel_id=1, source_target_pairs={{0,4},{4,8},{8,12},{12,16},{16,20},{20,24},{24,28},{28,0},{1,5},{5... | collective-permute-start | bytes 393224 | tf_op jit(solution)/shard_map/ppermute | solution.py:56
  42.5 8.2 %collective-permute-start.4 = (bf16[2,128,256]{1,2,0:T(8,128)(2,1)S(1)}, bf16[2,128,256]{1,2,0:T(8,128)(2,1)S(1)}, u32[]{:S(2)}, u32[]{:S(2)}) collective-permute-start(bf16[2,128,256]{1,2,0:T(8,128)(2,1)S(1)} %collective-permute-done.3), channel_id=1, source_target_pairs={{0,4},{4,8},{8,12},{12,16},{16,20},{20,24},{24,28},{28,0},{1,5},{5... | collective-permute-start | bytes 393224 | tf_op jit(solution)/shard_map/ppermute | solution.py:56
  50.7 8.8 %collective-permute-start.5 = (bf16[2,128,256]{1,2,0:T(8,128)(2,1)S(1)}, bf16[2,128,256]{1,2,0:T(8,128)(2,1)S(1)}, u32[]{:S(2)}, u32[]{:S(2)}) collective-permute-start(bf16[2,128,256]{1,2,0:T(8,128)(2,1)S(1)} %collective-permute-done.4), channel_id=1, source_target_pairs={{0,4},{4,8},{8,12},{12,16},{16,20},{20,24},{24,28},{28,0},{1,5},{5... | collective-permute-start | bytes 393224 | tf_op jit(solution)/shard_map/ppermute | solution.py:56
  59.5 8.8 %collective-permute-start.6 = (bf16[2,128,256]{1,2,0:T(8,128)(2,1)S(1)}, bf16[2,128,256]{1,2,0:T(8,128)(2,1)S(1)}, u32[]{:S(2)}, u32[]{:S(2)}) collective-permute-start(bf16[2,128,256]{1,2,0:T(8,128)(2,1)S(1)} %collective-permute-done.5), channel_id=1, source_target_pairs={{0,4},{4,8},{8,12},{12,16},{16,20},{20,24},{24,28},{28,0},{1,5},{5... | collective-permute-start | bytes 393224 | tf_op jit(solution)/shard_map/ppermute | solution.py:56
  68.7 0.8 copy-start.7
  69.0 0.9 copy-start.10
  70.2 3.6 copy-start.8
  70.2 4.0 copy-start.12
  70.6 2.6 copy-start.5
  70.7 23.9 %copy-start.2 = (bf16[128,512]{1,0:T(8,128)(2,1)S(1)}, bf16[128,512]{1,0:T(8,128)(2,1)}, u32[]{:S(2)}) copy-start(bf16[128,512]{1,0:T(8,128)(2,1)} %param.22) | copy-start | bytes 393220
  73.2 160.1 %all-gather.7.cloned.1.call-start = ((), (), s32[]{:S(2)}) async-start(), calls=%async_computation.6 | async-start | bytes 3244032 | tf_op jit(solution)/shard_map/all_gather | solution.py:114
  109.6 123.7 %copy-start.1 = (bf16[128,2048]{1,0:T(8,128)(2,1)}, bf16[128,2048]{1,0:T(8,128)(2,1)S(1)}, u32[]{:S(2)}) copy-start(bf16[128,2048]{1,0:T(8,128)(2,1)S(1)} %all_gather.16) | copy-start | bytes 1572868
  113.9 100.5 %all-to-all-start = ((bf16[8,96,2048]{2,1,0:T(8,128)(2,1)}), bf16[8,96,2048]{2,1,0:T(8,128)(2,1)}, u32[]{:S(2)}, u32[]{:S(2)}) async-start(bf16[8,96,2048]{2,1,0:T(8,128)(2,1)} %bitcast.109), calls=%async_computation.1 | async-start | bytes 6291456 | tf_op jit(solution)/shard_map/all_to_all | solution.py:144
  119.4 225.2 %all-gather.11.cloned.1.call-start = ((), (), s32[]{:S(2)}) async-start(), calls=%async_computation.8 | async-start | bytes 3244032 | tf_op jit(solution)/shard_map/all_gather | solution.py:125
  227.0 5.4 %copy-start.9 = (bf16[2048]{0:T(1024)(128)(2,1)S(1)}, bf16[2048]{0:T(1024)(128)(2,1)}, u32[]{:S(2)}) copy-start(bf16[2048]{0:T(1024)(128)(2,1)} %param.28) | copy-start | bytes 12292
  227.1 5.4 %copy-start.11 = (f32[128,4]{0,1:T(4,128)S(1)}, f32[128,4]{0,1:T(4,128)}, u32[]{:S(2)}) copy-start(f32[128,4]{0,1:T(4,128)} %param.33) | copy-start | bytes 6148
  227.1 102.8 %all-to-all-start.1 = ((bf16[8,96,2048]{2,1,0:T(8,128)(2,1)}), bf16[8,96,2048]{2,1,0:T(8,128)(2,1)}, u32[]{:S(2)}, u32[]{:S(2)}) async-start(bf16[8,96,2048]{2,1,0:T(8,128)(2,1)} %bitcast.110), calls=%async_computation.2 | async-start | bytes 6291456 | tf_op jit(solution)/shard_map/all_to_all | solution.py:153
  231.6 140.7 %all-gather.9.cloned.1.call-start = ((), (), s32[]{:S(2)}) async-start(), calls=%async_computation.7 | async-start | bytes 3244032 | tf_op jit(solution)/shard_map/all_gather | solution.py:119
  232.2 168.2 %reduce-scatter.5.cloned.1.call-start = ((), (), s32[]{:S(2)}) async-start(), calls=%async_computation.9 | async-start | bytes 655360 | tf_op jit(solution)/shard_map/reduce_scatter | solution.py:169
  372.3 8.1 %copy-start.6 = (bf16[128,2,128]{0,2,1:T(8,128)(2,1)S(1)}, bf16[128,2,128]{0,2,1:T(8,128)(2,1)}, u32[]{:S(2)}) copy-start(bf16[128,2,128]{0,2,1:T(8,128)(2,1)} %copy-done.5) | copy-start | bytes 196612
  372.3 28.1 %copy-start.3 = (bf16[128,512]{1,0:T(8,128)(2,1)S(1)}, bf16[128,512]{1,0:T(8,128)(2,1)}, u32[]{:S(2)}) copy-start(bf16[128,512]{1,0:T(8,128)(2,1)} %param.22) | copy-start | bytes 393220
  372.3 28.1 %copy-start.4 = (bf16[128,512]{1,0:T(8,128)(2,1)S(1)}, bf16[128,512]{1,0:T(8,128)(2,1)}, u32[]{:S(2)}) copy-start(bf16[128,512]{1,0:T(8,128)(2,1)} %reduce-scatter.3.cloned.1.call-done) | copy-start | bytes 393220
Sparse Core Ops, SparseCore 0:
  26.6 43.2 all-gather.4
  73.3 21.1 reduce-scatter.2
  96.8 109.6 all-gather.6
  208.5 102.8 all-gather.10
  313.5 58.7 all-gather.8
  380.6 19.8 reduce-scatter.4
